TPU v7x, 32 devices: a whole 2x2x4 slice. The times are simulated.
32 devices in a mesh: groups: 2 (over y), gx: 16 (over z, x, core).
Axes of the slice: x: 2, y: 2, z: 4, core: 2. Of those that a mesh axis runs over, the one named last changes fastest.
Arguments:
- initial: float32 [20, 4, 256, 1024], P('groups', None, 'gx'), parts along dimension 0, may hold values from -6 to 6
- background: float32 [20, 4, 256, 1024], P('groups', None, 'gx'), parts along dimension 0, may hold values from -6.5 to 6.5
- mixing: float32 [40, 40], replicated, may hold values from -1 to 1
- diffusion: float32 [10, 4], replicated, may hold values from 0.03 to 0.2
- advection: float32 [2, 10, 4], replicated, may hold values from -0.1 to 0.1
- obs_values: float32 [4, 4096], P('groups', 'gx'), parts along dimension 0, may hold values from -6 to 6
- obs_weight: float32 [2, 4096], P('groups', 'gx'), parts along dimension 0, may hold values from 0.5 to 4
- interp_weights: float32 [8, 4096], P('groups', 'gx'), parts along dimension 0, may hold values from 0.1 to 1
- stencil_index: int32 [8, 4096], P('groups', 'gx'), parts along dimension 0, may hold values from 0 to 655359, as said below
- station_tile: int32 [4096, 2], P('gx', 'groups'), parts along dimension 1, may hold values from 0 to 15; in each aligned block of 256 rows (0 to 255, 256 to 511, ...) at most 24 rows name the same one
- counts: int32 [2, 16], P('groups', 'gx'), parts along dimension 0, may hold values from 1 to 256, 3072 in all within a row
Outputs:
- gradient: float32 [20, 4, 256, 1024], P('groups', None, 'gx'), parts along dimension 0
There are 2 independent parts, one for each index of `groups`. A program takes and returns all parts, laid end to end along the dimension named above; an argument that names none is the same for every part. Nothing has to cross between parts.
Inputs may be any that keep to these rules, and one draw needn't show every extreme that they name: `station_tile`: within the rows of one device, no tile is named more than 24 times; some tile is named exactly 24 times in some or all devices' rows. Live observations of a tile occupy its first counts slots; some tile has 256. `stencil_index`: each column holds four cells of one channel of the owner tile, a cell being (channel * 16 + row) * 1024 + column: (row, column), (row, column + 1), (row + 1, column), (row + 1, column + 1) in that order.
All inputs are finite; a program needn't handle non-finite values. No bound on the sum of `counts` on one device may be relied on, other than what follows from the above.
Results may differ from a plain program's by a relative error of at most 0.00014.
Values sent between devices are 32-bit elements; how exact they have to be, the bound alone decides.
A program may use at most 64 MiB of HBM per device.

v0:
```python
import functools
import jax
import jax.numpy as jnp
from jax import lax
from jax.experimental import pallas as pl
from jax.experimental.pallas import tpu as pltpu
from jax.sharding import PartitionSpec as P

MESH = pl.DeviceIdType.MESH
WIN = 256


def fdot(a, b, dims):
    return lax.dot_general(a, b, (dims, ((), ())), preferred_element_type=jnp.float32)


def split3(v):
    hi = v.astype(jnp.bfloat16)
    rest = v - hi.astype(jnp.float32)
    mid = rest.astype(jnp.bfloat16)
    lo = (rest - mid.astype(jnp.float32)).astype(jnp.bfloat16)
    return hi, mid, lo


def widen_mix(m):
    hi = m.astype(jnp.bfloat16)
    lo = (m - hi.astype(jnp.float32)).astype(jnp.bfloat16)
    return jnp.concatenate([hi, hi, lo], axis=1)


def mix_rows(wide, v):
    hi = v.astype(jnp.bfloat16).astype(jnp.float32)
    parts = jnp.concatenate([hi, v - hi, hi], axis=0).astype(jnp.bfloat16)
    return fdot(wide, parts, ((1,), (0,)))


def shifts(v):
    cols = v.shape[1]
    lane = lax.broadcasted_iota(jnp.int32, (v.shape[0], 128), 1)
    east, west = pltpu.roll(v, cols - 1, 1), pltpu.roll(v, 1, 1)
    last = jnp.where(lane == 127, 0.0, east[:, cols - 128:])
    start = jnp.where(lane == 0, 0.0, west[:, :128])
    east = jnp.concatenate([east[:, :cols - 128], last], axis=1)
    west = jnp.concatenate([start, west[:, 128:]], axis=1)
    return east, west


def step_rows(centre, above, below, coef):
    east, west = shifts(centre)
    return (
        coef[0] * centre + coef[1] * above + coef[2] * below + coef[3] * east + coef[4] * west
    )


def exact_dot(hot, v, dims):
    hi, mid, lo = split3(v)
    return fdot(hot, hi, dims) + fdot(hot, mid, dims) + fdot(hot, lo, dims)


def hot_of(condition):
    return condition.astype(jnp.float32).astype(jnp.bfloat16)


def coef_columns(coef_ref, sign):
    c, a, b = coef_ref[:, 0:1], sign * coef_ref[:, 1:2], sign * coef_ref[:, 2:3]
    return 1.0 - 4.0 * c, c + a, c - a, c + b, c - b


def channel_column(table, chans):
    levels, fields = table.shape
    row = lax.broadcasted_iota(jnp.int32, (chans, fields), 0)
    field = lax.broadcasted_iota(jnp.int32, (chans, fields), 1)
    total = None
    for level in range(levels):
        hot = hot_of(row == field * levels + level)
        part = exact_dot(hot, table, ((1,), (1,)))[:, level:level + 1]
        total = part if total is None else total + part
    return total


def window_weights(column, weights, cols):
    block = jnp.minimum(jnp.floor(column * (1.0 / 128)), float(cols // 128 - 2))
    local = column - 128.0 * block
    lane = lax.broadcasted_iota(jnp.int32, (column.shape[0], WIN), 1).astype(jnp.float32)
    left, right = lane == local, lane == local + 1.0
    top = jnp.where(left, weights[0], 0.0) + jnp.where(right, weights[1], 0.0)
    low = jnp.where(left, weights[2], 0.0) + jnp.where(right, weights[3], 0.0)
    return top, low


def split_cell(cell, rows, cols):
    chan = jnp.floor(cell * (1.0 / (rows * cols)))
    rest = cell - chan * (rows * cols)
    line = jnp.floor(rest * (1.0 / cols))
    return line, chan, rest - line * cols


def place_rows(line, chan, column, count, cols):
    block = jnp.minimum(jnp.floor(column * (1.0 / 128)), float(cols // 128 - 2)) * 128.0
    zero = jnp.zeros_like(line)
    return jnp.concatenate([line, chan, block, count] + [zero] * 4, axis=0).astype(jnp.int32)


def forward_kernel(
    tiles, cap, vals, wts, interp, cells, target, count, diffusion, advection, mixing, u0,
    q1, mine, near, coef_out, mixing_t,
    send, recv, su0, su1, su2, sq1, hots, outbox,
    in_sem, out_sem, send_sem, recv_sem, halo_send, halo_recv, near_send, near_recv,
):
    me = lax.axis_index("gx")
    chans, rows, cols = u0.shape
    held = target.shape[1]
    slots = tiles * cap
    nt = ((1,), (1,))
    loads = [
        pltpu.make_async_copy(u0.at[:, r, :], su0.at[r + 2], in_sem.at[r]) for r in range(rows)
    ]
    for copy in loads:
        copy.start()
    barrier = pltpu.get_barrier_semaphore()

    def greet(d, _):
        pl.semaphore_signal(
            barrier, inc=1, device_id={"gx": lax.rem(me + d, tiles)}, device_id_type=MESH
        )
        return 0

    lax.fori_loop(1, tiles, greet, 0)
    names = target[...]
    match = (lax.broadcasted_iota(jnp.int32, (tiles, held), 0) == names).astype(jnp.float32)
    before = hot_of(
        lax.broadcasted_iota(jnp.int32, (held, held), 0)
        < lax.broadcasted_iota(jnp.int32, (held, held), 1)
    )
    ranks = fdot(match.astype(jnp.bfloat16), before, ((1,), (0,)))
    rank = jnp.sum(match * ranks, axis=0, keepdims=True).astype(jnp.int32)
    position = names * cap + rank
    hot = hot_of(lax.broadcasted_iota(jnp.int32, (slots, held), 0) == position)
    live = lax.broadcasted_iota(jnp.int32, (1, held), 1) < count[0, 0]
    weight = jnp.where(live, wts[...], 0.0)
    recs = jnp.concatenate(
        [vals[...], weight, interp[...], cells[0:1, :].astype(jnp.float32),
         jnp.zeros((120, held), jnp.float32)], axis=0)
    send[...] = exact_dot(hot, recs, nt).reshape(tiles, cap, 128)
    pl.semaphore_wait(barrier, tiles - 1)

    def edge(up, k):
        if up:
            src, dst, at, to = rows - 2 + k, k, k, me + 1
        else:
            src, dst, at, to = k, rows + 2 + k, 2 + k, me - 1
        return pltpu.make_async_remote_copy(
            src_ref=u0.at[:, src, :], dst_ref=su0.at[dst],
            send_sem=halo_send.at[at], recv_sem=halo_recv.at[at],
            device_id={"gx": to}, device_id_type=MESH)

    def parcel(d, to, row):
        return pltpu.make_async_remote_copy(
            src_ref=send.at[to], dst_ref=recv.at[row],
            send_sem=send_sem.at[d], recv_sem=recv_sem.at[d],
            device_id={"gx": to}, device_id_type=MESH)

    def start(d, _):
        parcel(d, lax.rem(me + d, tiles), me).start()
        return 0

    def finish(d, _):
        parcel(d, lax.rem(me + d, tiles), me).wait_send()
        source = lax.rem(me + tiles - d, tiles)
        parcel(d, source, source).wait_recv()
        return 0

    lax.fori_loop(1, tiles, start, 0)

    @pl.when(me < tiles - 1)
    def _():
        edge(True, 1).start()
        edge(True, 0).start()

    @pl.when(me > 0)
    def _():
        edge(False, 0).start()
        edge(False, 1).start()

    recv[me] = send[me]
    columns = [channel_column(t, chans) for t in (diffusion[...], advection[0], advection[1])]
    lane = lax.broadcasted_iota(jnp.int32, (chans, 128), 1)
    coef_out[...] = jnp.where(
        lane == 0, columns[0], jnp.where(lane == 1, columns[1], columns[2]))
    mixing_t[...] = mixing[...].T
    wide = widen_mix(mixing[...])
    coefs = coef_columns(coef_out, 1.0)

    def first(i, _):
        centre = su0[i + 1]
        su1[i] = step_rows(centre, su0[i + 2], su0[i], coefs) + mix_rows(wide, jnp.tanh(centre))
        return 0

    for copy in loads:
        copy.wait()
    lax.fori_loop(2, rows, first, 0)

    lax.fori_loop(1, tiles, finish, 0)
    records = recv[...].reshape(slots, 128)
    turned = records.T
    weights = turned[2:3, :]
    line, chan, column = split_cell(turned[7:8, :], rows, cols)
    ahead = hot_of(
        lax.broadcasted_iota(jnp.int32, (slots, slots), 0)
        < lax.broadcasted_iota(jnp.int32, (slots, slots), 1)
    )
    alive = (weights > 0.0).astype(jnp.float32)
    masks = jnp.concatenate(
        [alive, jnp.where(line >= rows - 3, alive, 0.0), jnp.where(line <= 1.0, alive, 0.0),
         jnp.zeros((5, slots), jnp.float32)], axis=0)
    order = fdot(masks.astype(jnp.bfloat16), ahead, ((1,), (0,)))
    spot = jnp.where(masks > 0.0, order, -1.0).astype(jnp.int32)
    totals = jnp.sum(masks, axis=1, keepdims=True)
    slot = lax.broadcasted_iota(jnp.int32, (slots, slots), 0)
    for k in range(3):
        hots[k] = hot_of(slot == spot[k:k + 1, :])

    @pl.when(me < tiles - 1)
    def _():
        for k in range(2):
            edge(True, k).wait_send()
            edge(False, k).wait_recv()

    @pl.when(me > 0)
    def _():
        for k in range(2):
            edge(False, k).wait_send()
            edge(True, k).wait_recv()

    blank = jnp.zeros((chans, cols), jnp.float32)

    @pl.when(me == 0)
    def _():
        su0[0] = blank
        su0[1] = blank

    @pl.when(me == tiles - 1)
    def _():
        su0[rows + 2] = blank
        su0[rows + 3] = blank

    def outer(k, _):
        return first(jnp.where(k < 2, k, rows - 2 + k), 0)

    lax.fori_loop(0, 4, outer, 0)

    @pl.when(me == 0)
    def _():
        su1[0] = blank

    @pl.when(me == tiles - 1)
    def _():
        su1[rows + 1] = blank

    stores = lambda i: pltpu.make_async_copy(sq1.at[i], q1.at[i], out_sem.at[i])

    def second(i, _):
        centre = su1[i + 1]
        th = jnp.tanh(centre)
        sq1[i + 1] = 1.0 - th * th
        stores(i + 1).start()
        su2[i] = step_rows(centre, su1[i + 2], su1[i], coefs) + mix_rows(wide, th)
        return 0

    for i in (0, rows + 1):
        th = jnp.tanh(su1[i])
        sq1[i] = 1.0 - th * th
        stores(i).start()
    lax.fori_loop(0, rows, second, 0)
    col = lambda k: records[:, k:k + 1]
    line_c, chan_c, column_c = split_cell(col(7), rows, cols)
    span = (rows - 1) * chans
    flat = lax.broadcasted_iota(jnp.int32, (slots, span), 1).astype(jnp.float32)
    pick = hot_of(flat == line_c * chans + chan_c)
    pick = jnp.concatenate([pick, pick], axis=1)

    def picked(state, first_row, start):
        block = state[first_row:first_row + rows - 1, :, start:start + WIN].reshape(span, WIN)
        hi = block.astype(jnp.bfloat16).astype(jnp.float32)
        both = jnp.concatenate([hi, block - hi], axis=0).astype(jnp.bfloat16)
        return fdot(pick, both, ((1,), (0,)))

    samples = [jnp.zeros((slots, 1), jnp.float32)] * 2
    lane = lax.broadcasted_iota(jnp.int32, (slots, WIN), 1).astype(jnp.float32)
    for start in range(0, cols, WIN):
        local = column_c - float(start)
        left, right = lane == local, lane == local + 1.0
        top = jnp.where(left, col(3), jnp.where(right, col(4), 0.0))
        low = jnp.where(left, col(5), jnp.where(right, col(6), 0.0))
        for which, (state, base) in enumerate(((su1, 1), (su2, 0))):
            found = picked(state, base, start) * top + picked(state, base + 1, start) * low
            samples[which] = samples[which] + jnp.sum(found, axis=1, keepdims=True)
    results = [col(2) * (samples[k] - col(k)) for k in range(2)]
    lane = lax.broadcasted_iota(jnp.int32, records.shape, 1)
    merged = jnp.where(lane == 0, results[0], jnp.where(lane == 1, results[1], 0.0)).T
    zero = jnp.zeros((7, slots), jnp.float32)
    for k, moved in ((1, -rows), (2, rows), (0, 0)):
        fields = jnp.concatenate(
            [merged[0:2, :], line + float(moved), turned[3:7, :], chan, column, zero], axis=0)
        hi, mid, lo = split3(fields)
        packed = fdot(hi, hots[k], nt) + fdot(mid, hots[k], nt) + fdot(lo, hots[k], nt)
        field = lax.broadcasted_iota(jnp.int32, packed.shape, 0)
        packed = jnp.where(field == 9, totals[k:k + 1, :], packed)
        if k == 0:
            mine[...] = packed
        else:
            outbox[k - 1] = packed

    def note(k):
        return pltpu.make_async_remote_copy(
            src_ref=outbox.at[k], dst_ref=near.at[k],
            send_sem=near_send.at[k], recv_sem=near_recv.at[k],
            device_id={"gx": me + 1 if k == 0 else me - 1}, device_id_type=MESH)

    @pl.when(me < tiles - 1)
    def _():
        note(0).start()

    @pl.when(me > 0)
    def _():
        note(1).start()

    for i in range(rows + 2):
        stores(i).wait()

    @pl.when(me == 0)
    def _():
        near[0] = jnp.zeros((16, slots), jnp.float32)

    @pl.when(me == tiles - 1)
    def _():
        near[1] = jnp.zeros((16, slots), jnp.float32)

    @pl.when(me < tiles - 1)
    def _():
        note(0).wait_send()
        note(1).wait_recv()

    @pl.when(me > 0)
    def _():
        note(1).wait_send()
        note(0).wait_recv()


def adjoint_kernel(
    tiles, u0, ub, q1, mine, near, mixing_t, coef, out,
    su0, sub, sq1, f1, f2, sout, parts, place_v, place_s, in_sem, place_sem, out_sem,
):
    me = lax.axis_index("gx")
    chans, rows, cols = u0.shape
    slots = mine.shape[1]
    load_q = [pltpu.make_async_copy(q1.at[i], sq1.at[i], in_sem.at[0, i]) for i in range(rows + 2)]
    load_u = [pltpu.make_async_copy(u0.at[:, i, :], su0.at[i], in_sem.at[1, i]) for i in range(rows)]
    load_b = [pltpu.make_async_copy(ub.at[:, i, :], sub.at[i], in_sem.at[2, i]) for i in range(rows)]
    lists = [mine[...], near[0], near[1]]
    for group, block in enumerate(lists):
        place_v[group] = place_rows(
            block[2:3, :] + 3.0, block[7:8, :], block[8:9, :], block[9:10, :], cols)
    placing = pltpu.make_async_copy(place_v, place_s, place_sem)
    placing.start()
    for copy in load_q + load_u + load_b:
        copy.start()

    def clear(i, _):
        f1[i] = jnp.zeros((chans, cols), jnp.float32)
        f2[i] = jnp.zeros((chans, cols), jnp.float32)
        return 0

    lax.fori_loop(0, rows + 6, clear, 0)
    placing.wait()
    for group in range(3):
        amount = place_s[group, 3, 0]
        for start in range(0, slots, 128):

            @pl.when(amount > start)
            def _():
                block = (mine if group == 0 else near.at[group - 1])[:, start:start + 128]
                full = jnp.concatenate([block, jnp.zeros((112, 128), jnp.float32)], axis=0).T
                col = lambda k: full[:, k:k + 1]
                top, low = window_weights(col(8), [col(3 + k) for k in range(4)], cols)
                parts[0] = col(0) * top
                parts[1] = col(0) * low
                parts[2] = col(1) * top
                parts[3] = col(1) * low

                def add(j2, _):
                    for k in range(2):
                        j = j2 * 2 + k
                        at, ch = place_s[group, 0, start + j], place_s[group, 1, start + j]
                        block = pl.multiple_of(place_s[group, 2, start + j], 128)
                        spots = [
                            (ref, (at + step, pl.ds(ch, 1), pl.ds(block, WIN)), 2 * t + step)
                            for t, ref in enumerate((f1, f2)) for step in range(2)]
                        sums = [
                            ref[spot] + parts[part, pl.ds(j, 1), :] for ref, spot, part in spots]
                        for (ref, spot, _), total in zip(spots, sums):
                            ref[spot] = total
                    return 0

                lax.fori_loop(0, (jnp.minimum(amount - start, 128) + 1) // 2, add, 0)

    wide = widen_mix(mixing_t[...])
    coefs = coef_columns(coef, -1.0)
    for copy in load_q:
        copy.wait()

    def first(i, _):
        centre = f2[i + 2]
        spread = step_rows(centre, f2[i + 3], f2[i + 1], coefs)
        f1[i + 2] = f1[i + 2] + spread + sq1[i] * mix_rows(wide, centre)
        return 0

    lax.fori_loop(0, rows + 2, first, 0)

    @pl.when(me == 0)
    def _():
        f1[2] = jnp.zeros((chans, cols), jnp.float32)

    @pl.when(me == tiles - 1)
    def _():
        f1[rows + 3] = jnp.zeros((chans, cols), jnp.float32)

    for copy in load_u + load_b:
        copy.wait()
    save = lambda i: pltpu.make_async_copy(sout.at[i], out.at[:, i, :], out_sem.at[i])
    for i in range(rows):
        centre = f1[i + 3]
        state = su0[i]
        th = jnp.tanh(state)
        sout[i] = (
            (state - sub[i])
            + step_rows(centre, f1[i + 4], f1[i + 2], coefs)
            + (1.0 - th * th) * mix_rows(wide, centre)
        )
        save(i).start()
    for i in range(rows):
        save(i).wait()


def shards(
    initial, background, mixing, diffusion, advection, obs_values, obs_weight,
    interp_weights, stencil_index, station_tile, counts,
):
    num_fields, num_levels, rows, cols = initial.shape
    chans = num_fields * num_levels
    tiles = lax.axis_size("gx")
    held = obs_values.shape[1]
    most = max(2, held * 3 // (2 * tiles))
    cap = -(-most // 8) * 8
    slots = tiles * cap
    u0 = initial.reshape(chans, rows, cols)
    ub = background.reshape(chans, rows, cols)
    f32, i32 = jnp.float32, jnp.int32
    anyspace = pl.BlockSpec(memory_space=pl.ANY)
    vmem = pl.BlockSpec(memory_space=pltpu.VMEM)
    smem = pl.BlockSpec(memory_space=pltpu.SMEM)
    dma = pltpu.SemaphoreType.DMA
    limit = 60 * 1024 * 1024
    shape = jax.ShapeDtypeStruct
    q1, mine, near, coef, mixing_t = pl.pallas_call(
        functools.partial(forward_kernel, tiles, cap),
        out_shape=(
            shape((rows + 2, chans, cols), f32),
            shape((16, slots), f32),
            shape((2, 16, slots), f32),
            shape((chans, 128), f32),
            shape((chans, chans), f32),
        ),
        in_specs=[vmem] * 5 + [smem] + [vmem] * 3 + [anyspace],
        out_specs=(anyspace, vmem, vmem, vmem, vmem),
        scratch_shapes=[
            pltpu.VMEM((tiles, cap, 128), f32),
            pltpu.VMEM((tiles, cap, 128), f32),
            pltpu.VMEM((rows + 4, chans, cols), f32),
            pltpu.VMEM((rows + 2, chans, cols), f32),
            pltpu.VMEM((rows, chans, cols), f32),
            pltpu.VMEM((rows + 2, chans, cols), f32),
            pltpu.VMEM((3, slots, slots), jnp.bfloat16),
            pltpu.VMEM((2, 16, slots), f32),
            dma((rows,)),
            dma((rows + 2,)),
            dma((tiles,)),
            dma((tiles,)),
            dma((4,)),
            dma((4,)),
            dma((2,)),
            dma((2,)),
        ],
        compiler_params=pltpu.CompilerParams(
            collective_id=0, has_side_effects=True, vmem_limit_bytes=limit),
    )(obs_values, obs_weight, interp_weights, stencil_index,
      station_tile.reshape(1, held), counts, diffusion.T, advection.transpose(0, 2, 1),
      mixing, u0)
    gradient = pl.pallas_call(
        functools.partial(adjoint_kernel, tiles),
        out_shape=shape((chans, rows, cols), f32),
        in_specs=[anyspace, anyspace, anyspace, vmem, vmem, vmem, vmem],
        out_specs=anyspace,
        scratch_shapes=[
            pltpu.VMEM((rows, chans, cols), f32),
            pltpu.VMEM((rows, chans, cols), f32),
            pltpu.VMEM((rows + 2, chans, cols), f32),
            pltpu.VMEM((rows + 6, chans, cols), f32),
            pltpu.VMEM((rows + 6, chans, cols), f32),
            pltpu.VMEM((rows, chans, cols), f32),
            pltpu.VMEM((4, 128, WIN), f32),
            pltpu.VMEM((3, 8, slots), i32),
            pltpu.SMEM((3, 8, slots), i32),
            dma((3, rows + 2)),
            dma,
            dma((rows,)),
        ],
        compiler_params=pltpu.CompilerParams(vmem_limit_bytes=limit),
    )(u0, ub, q1, mine, near, mixing_t, coef)
    return gradient.reshape(num_fields, num_levels, rows, cols)


def solution(mesh):
    placed = (
        P("groups", None, "gx", None),
        P("groups", None, "gx", None),
        P(),
        P(),
        P(),
        P("groups", "gx"),
        P("groups", "gx"),
        P("groups", "gx"),
        P("groups", "gx"),
        P("gx", "groups"),
        P("groups", "gx"),
    )
    return jax.shard_map(
        shards, mesh=mesh, in_specs=placed, out_specs=P("groups", None, "gx", None), check_vma=False
    )
```

profile of v0, /device:TPU:1, one launch (start us, length us, event | category | flops | bytes accessed | tf_op | source)
XLA Modules:
  0.0 47.7 jit_solution(1107936497468411901)
XLA Ops:
  0.7 32.3 %shard_map.109 = (f32[18,40,1024]{2,1,0:T(8,128)}, f32[16,384]{1,0:T(8,128)}, f32[2,16,384]{2,1,0:T(8,128)}, f32[40,128]{1,0:T(8,128)}, f32[40,40]{1,0:T(8,128)}) custom-call(f32[2,256]{1,0:T(2,128)} %vals.1, f32[1,256]{1,0:T(1,128)} %wts.1, f32[4,256]{1,0:T(4,128)} %interp.1, s32[4,256]{1,0:T(4,128)} %cells.1, s32[1,256]{1,0:T(1,128)} %bitcast.11, ...), custom_call_target="tpu_custom_call" | custom-call | tf_op jit(solution)/shard_map/pallas_call | solution.py:465
  33.0 14.5 %shard_map.110 = f32[40,16,1024]{2,1,0:T(8,128)} custom-call(f32[40,16,1024]{2,1,0:T(8,128)} %bitcast.7, f32[40,16,1024]{2,1,0:T(8,128)} %bitcast.8, f32[18,40,1024]{2,1,0:T(8,128)} %get-tuple-element.10.q1, f32[16,384]{1,0:T(8,128)} %get-tuple-element.11.mine, f32[2,16,384]{2,1,0:T(8,128)} %get-tuple-element.12.near, f32[40,40]{1,0:T(8,128)} %get-tuple-element.13.mixing_t, ...), custom_call_target="tpu_custom_call" | custom-call | tf_op jit(solution)/shard_map/pallas_call | solution.py:499
where the time goes:
time: 48.6 us; the launch traced here: 47.7 us
  Pallas kernels  46.8 us (96%)
  between operations  0.82 us (2%)
    pallas_call x1, Pallas kernels, shards(): pl.pallas_call(functools.partial(forward_kernel, tiles, cap), out_shape=(...  32.3 us
    pallas_call x1, Pallas kernels, shards(): pl.pallas_call(functools.partial(adjoint_kernel, tiles), out_shape=shape(...  14.5 us

commit v1 on v0

--- a/solution.py
+++ b/solution.py
@@ -198,7 +198,7 @@
 
     for copy in loads:
         copy.wait()
-    lax.fori_loop(2, rows, first, 0)
+    lax.fori_loop(2, rows, first, 0, unroll=2)
 
     lax.fori_loop(1, tiles, finish, 0)
     records = recv[...].reshape(slots, 128)
@@ -271,7 +271,7 @@
         th = jnp.tanh(su1[i])
         sq1[i] = 1.0 - th * th
         stores(i).start()
-    lax.fori_loop(0, rows, second, 0)
+    lax.fori_loop(0, rows, second, 0, unroll=2)
     col = lambda k: records[:, k:k + 1]
     line_c, chan_c, column_c = split_cell(col(7), rows, cols)
     span = (rows - 1) * chans
@@ -415,7 +415,7 @@
         f1[i + 2] = f1[i + 2] + spread + sq1[i] * mix_rows(wide, centre)
         return 0
 
-    lax.fori_loop(0, rows + 2, first, 0)
+    lax.fori_loop(0, rows + 2, first, 0, unroll=2)
 
     @pl.when(me == 0)
     def _():

time: 48.6 us -> 46.7 us (0.961)
  Pallas kernels: 46.8 us -> 45 us
    pallas_call x1, Pallas kernels: 14.5 us -> 13.4 us  [shards(): pl.pallas_call(functools.partial(adjoint_kernel, tiles), out_shape=shape(...]
    pallas_call x1, Pallas kernels: 32.3 us -> 31.6 us  [shards(): pl.pallas_call(functools.partial(forward_kernel, tiles, cap), out_shape=(...]
where the time goes in v1:
time: 46.7 us; the launch traced here: 45.8 us
  Pallas kernels  45 us (96%)
  between operations  0.82 us (2%)
    pallas_call x1, Pallas kernels, shards(): pl.pallas_call(functools.partial(forward_kernel, tiles, cap), out_shape=(...  31.6 us
    pallas_call x1, Pallas kernels, shards(): pl.pallas_call(functools.partial(adjoint_kernel, tiles), out_shape=shape(...  13.4 us

profile of v1, /device:TPU:1, one launch (start us, length us, event | category | flops | bytes accessed | tf_op | source)
XLA Modules:
  0.0 45.8 jit_solution(4207422125481336607)
XLA Ops:
  0.7 31.6 %shard_map.109 = (f32[18,40,1024]{2,1,0:T(8,128)}, f32[16,384]{1,0:T(8,128)}, f32[2,16,384]{2,1,0:T(8,128)}, f32[40,128]{1,0:T(8,128)}, f32[40,40]{1,0:T(8,128)}) custom-call(f32[2,256]{1,0:T(2,128)} %vals.1, f32[1,256]{1,0:T(1,128)} %wts.1, f32[4,256]{1,0:T(4,128)} %interp.1, s32[4,256]{1,0:T(4,128)} %cells.1, s32[1,256]{1,0:T(1,128)} %bitcast.11, ...), custom_call_target="tpu_custom_call" | custom-call | tf_op jit(solution)/shard_map/pallas_call | solution.py:465
  32.3 13.4 %shard_map.110 = f32[40,16,1024]{2,1,0:T(8,128)} custom-call(f32[40,16,1024]{2,1,0:T(8,128)} %bitcast.7, f32[40,16,1024]{2,1,0:T(8,128)} %bitcast.8, f32[18,40,1024]{2,1,0:T(8,128)} %get-tuple-element.10.q1, f32[16,384]{1,0:T(8,128)} %get-tuple-element.11.mine, f32[2,16,384]{2,1,0:T(8,128)} %get-tuple-element.12.near, f32[40,40]{1,0:T(8,128)} %get-tuple-element.13.mixing_t, ...), custom_call_target="tpu_custom_call" | custom-call | tf_op jit(solution)/shard_map/pallas_call | solution.py:499
